TPU v7x, 512 devices: a whole 4x4x16 slice. The times are simulated.
512 devices in a mesh: slab: 32 (over y, z_hi, x), shots: 16 (over z_lo, core).
Axes of the slice: x: 4, y: 4, z: 16 (z_hi: 2, z_lo: 8; z = z_hi * 8 + z_lo), core: 2. Of those that a mesh axis runs over, the one named last changes fastest.
Arguments:
- src_prev: float32 [32, 256, 64, 128], P('shots', 'slab'), may hold values from -6 to 6
- src_cur: float32 [32, 256, 64, 128], P('shots', 'slab'), may hold values from -6 to 6
- rcv_prev: float32 [32, 256, 64, 128], P('shots', 'slab'), may hold values from -6 to 6
- rcv_cur: float32 [32, 256, 64, 128], P('shots', 'slab'), may hold values from -6 to 6
- velocity: float32 [256, 64, 128], P('slab'), may hold values from 0.05 to 0.18
- wavelet: float32 [2, 32], P(None, 'shots'), may hold values from -6 to 6
- residual_traces: float32 [2, 32, 256], P(None, 'shots'), may hold values from -6 to 6
- source_depth: int32 [32], P('shots'), may hold values from 0 to 255
- source_y: int32 [32], P('shots'), may hold values from 21 to 42
- source_x: int32 [32], P('shots'), may hold values from 42 to 85
- half_y: int32 [32], P('shots'), may hold values from 10 to 21
- half_x: int32 [32], P('shots'), may hold values from 21 to 42
- receiver_cell: int32 [32, 256], P('shots'), may hold values from 0 to 2097151
Outputs:
- src_last: float32 [32, 256, 64, 128], P('shots', 'slab')
- rcv_last: float32 [32, 256, 64, 128], P('shots', 'slab')
- image: float32 [256, 64, 128], P('slab')
All inputs are finite; a program needn't handle non-finite values.
Results may differ from a plain program's by a relative error of at most 0.0003.
Values sent between devices are 32-bit elements; how exact they have to be, the bound alone decides.
A program may use at most 64 MiB of HBM per device.

v0:
```python
import jax
import jax.numpy as jnp
from jax import lax
from jax.sharding import PartitionSpec as P

STEPS = 2
COEF = (-205.0 / 72.0, 8.0 / 5.0, -1.0 / 5.0, 8.0 / 315.0, -1.0 / 560.0)


def extended(block, sides, width):
    for axis, dim in sides:
        count = lax.axis_size(axis)
        forward = [(i, i + 1) for i in range(count - 1)]
        backward = [(target, source) for source, target in forward]
        low = lax.ppermute(
            lax.slice_in_dim(block, block.shape[dim] - width, None, axis=dim), axis, forward
        )
        high = lax.ppermute(lax.slice_in_dim(block, 0, width, axis=dim), axis, backward)
        block = jnp.concatenate([low, block, high], axis=dim)
    return block


def laplace(padded):
    axis_z = padded.ndim - 3
    length = padded.shape[axis_z] - 8
    center = lax.slice_in_dim(padded, 4, 4 + length, axis=axis_z)
    total = 3.0 * COEF[0] * center
    for shift_k in range(1, 5):
        upper = lax.slice_in_dim(padded, 4 + shift_k, 4 + shift_k + length, axis=axis_z)
        lower = lax.slice_in_dim(padded, 4 - shift_k, 4 - shift_k + length, axis=axis_z)
        total = total + COEF[shift_k] * (upper + lower)
    widths = [(0, 0)] * (center.ndim - 2) + [(4, 4), (4, 4)]
    plane = jnp.pad(center, widths)
    rows_y = center.shape[-2]
    cols_x = center.shape[-1]
    for shift_k in range(1, 5):
        side_y = (
            plane[..., 4 + shift_k : 4 + shift_k + rows_y, 4 : 4 + cols_x]
            + plane[..., 4 - shift_k : 4 - shift_k + rows_y, 4 : 4 + cols_x]
        )
        side_x = (
            plane[..., 4 : 4 + rows_y, 4 + shift_k : 4 + shift_k + cols_x]
            + plane[..., 4 : 4 + rows_y, 4 - shift_k : 4 - shift_k + cols_x]
        )
        total = total + COEF[shift_k] * (side_y + side_x)
    return total


def band_mask(source_y, source_x, half_y, half_x, rows_y, cols_x):
    grid_y = jnp.arange(rows_y, dtype=jnp.int32)
    grid_x = jnp.arange(cols_x, dtype=jnp.int32)
    inside_y = jnp.abs(grid_y[None, :, None] - source_y[:, None, None]) <= half_y[:, None, None]
    inside_x = jnp.abs(grid_x[None, None, :] - source_x[:, None, None]) <= half_x[:, None, None]
    return (inside_y & inside_x).astype(jnp.float32)


def inject(cells, values, begin, length, rows_y, cols_x):
    plane = rows_y * cols_x
    depth = cells // plane
    rest = cells - depth * plane
    local = depth - begin
    valid = (local >= 0) & (local < length)
    flat = jnp.where(valid, local * plane + rest, 0)
    amounts = jnp.where(valid, values, jnp.zeros_like(values))
    count = cells.shape[0]
    rows = jnp.broadcast_to(jnp.arange(count, dtype=jnp.int32)[:, None], flat.shape)
    field = jnp.zeros((count, length * plane), jnp.float32).at[rows, flat].add(amounts)
    return field.reshape(count, length, rows_y, cols_x)


def per_device(
    src_prev,
    src_cur,
    rcv_prev,
    rcv_cur,
    velocity,
    wavelet,
    residual_traces,
    source_depth,
    source_y,
    source_x,
    half_y,
    half_x,
    receiver_cell,
):
    shot_count, depth, rows_y, cols_x = src_cur.shape
    start = lax.axis_index("slab") * depth
    mask = band_mask(source_y, source_x, half_y, half_x, rows_y, cols_x)[:, None]
    scells = (source_depth * rows_y * cols_x + source_y * cols_x + source_x)[:, None]
    terms = []
    up, u, vp, v = (src_prev, src_cur, rcv_prev, rcv_cur)
    for step in range(STEPS):
        stacked = jnp.stack([u, v])
        padded = extended(stacked, (("slab", 2),), 4)
        lap = laplace(padded)
        sdelta = inject(scells, wavelet[step][:, None], start, depth, rows_y, cols_x)
        rdelta = inject(receiver_cell, residual_traces[step], start, depth, rows_y, cols_x)
        sdelta, rdelta = (sdelta, rdelta)
        unew = mask * (2.0 * u - up + velocity * lap[0] + sdelta)
        vnew = mask * (2.0 * v - vp + velocity * lap[1] + rdelta)
        terms.append(jnp.sum((unew - 2.0 * u + up) * vnew, axis=0))
        up, u, vp, v = (u, unew, v, vnew)
    src_last, rcv_last = (u, v)
    local_sum = terms[0]
    for extra in terms[1:]:
        local_sum = local_sum + extra
    image = lax.psum(local_sum, "shots")
    return (src_last, rcv_last, image)


def solution(mesh):
    return jax.shard_map(
        per_device,
        mesh=mesh,
        in_specs=(
            P("shots", "slab", None, None),
            P("shots", "slab", None, None),
            P("shots", "slab", None, None),
            P("shots", "slab", None, None),
            P("slab", None, None),
            P(None, "shots"),
            P(None, "shots", None),
            P("shots"),
            P("shots"),
            P("shots"),
            P("shots"),
            P("shots"),
            P("shots", None),
        ),
        out_specs=(
            P("shots", "slab", None, None),
            P("shots", "slab", None, None),
            P("slab", None, None),
        ),
        check_vma=False,
    )
```

profile of v0, /device:TPU:1, one launch (start us, length us, event | category | flops | bytes accessed | tf_op | source)
XLA Modules:
  0.0 348.8 jit_solution(7300250642595813293)
XLA Ops:
  7.2 0.0 copy-start.7
  7.2 0.0 copy-start.6
  7.2 0.0 copy-start.8
  7.2 0.0 all-reduce.4.cloned.1.call-start
  7.3 2.3 fusion.58
  9.5 1.3 collective-permute-start
  10.8 4.6 %collective-permute-start.1 = (f32[2,2,4,64,128]{4,3,2,1,0:T(8,128)}, f32[2,2,4,64,128]{4,3,2,1,0:T(8,128)S(1)}, u32[]{:S(2)}, u32[]{:S(2)}) collective-permute-start(f32[2,2,4,64,128]{4,3,2,1,0:T(8,128)} %get-tuple-element.21), channel_id=1, source_target_pairs={{0,16},{16,32},{32,48},{48,64},{64,80},{80,96},{96,112},{112,128},... | collective-permute-start | bytes 1572872 | tf_op jit(solution)/shard_map/ppermute | solution.py:15
  15.6 0.1 copy.17
  15.7 0.2 fusion.83
  15.9 0.1 broadcast.180.clone.1
  16.1 0.6 scatter_fusion
  16.8 0.1 broadcast.180.clone
  16.9 0.0 copy-start.12
  16.9 0.0 copy-start
  16.9 0.0 copy-start.1
  16.9 24.8 %scatter_fusion.1 = f32[2,65536]{1,0:T(2,128)S(1)} fusion(f32[2,65536]{1,0:T(2,128)S(1)} %broadcast.180.clone, s32[512]{0:T(512)S(1)} %bitcast.87, f32[512]{0:T(512)S(1)} %bitcast.111), kind=kCustom, calls=%fused_computation.1 | custom fusion | flops 512 | bytes 10240 | tf_op jit(solution)/shard_map/scatter-add | solution.py:67
  41.7 0.0 copy-start.13
  41.8 0.1 abs_compare_fusion
  41.9 0.1 pad_maximum_fusion.2
  42.0 0.4 copy-done.13
  42.4 0.1 abs_compare_fusion.1
  42.5 0.1 and_convert_fusion
  42.6 0.0 collective-permute-done
  42.6 0.0 collective-permute-done.1
  42.6 0.4 pad_maximum_fusion
  43.0 0.0 copy-start.2
  43.0 0.0 copy-start.4
  43.0 0.0 copy-start.5
  43.0 2.5 fusion.6
  45.5 0.5 fusion.71
  46.0 1.0 fusion.56
  47.0 1.3 collective-permute-start.2
  48.3 4.8 %collective-permute-start.3 = (f32[2,2,4,64,128]{4,3,2,1,0:T(8,128)}, f32[2,2,4,64,128]{4,3,2,1,0:T(8,128)}, u32[]{:S(2)}, u32[]{:S(2)}) collective-permute-start(f32[2,2,4,64,128]{4,3,2,1,0:T(8,128)} %get-tuple-element.17), channel_id=1, source_target_pairs={{0,16},{16,32},{32,48},{48,64},{64,80},{80,96},{96,112},{112,128},... | collective-permute-start | bytes 1572872 | tf_op jit(solution)/shard_map/ppermute | solution.py:15
  53.1 0.1 broadcast.180.clone.3
  53.3 0.6 scatter_fusion.2
  54.0 0.1 broadcast.180.clone.2
  54.1 24.8 %scatter_fusion.3 = f32[2,65536]{1,0:T(2,128)S(1)} fusion(f32[2,65536]{1,0:T(2,128)S(1)} %broadcast.180.clone.2, s32[512]{0:T(512)S(1)} %bitcast.88, f32[512]{0:T(512)S(1)} %bitcast.110), kind=kCustom, calls=%fused_computation.3 | custom fusion | flops 512 | bytes 10240 | tf_op jit(solution)/shard_map/scatter-add | solution.py:67
  78.9 0.1 pad_maximum_fusion.3
  79.0 0.0 collective-permute-done.2
  79.0 0.0 collective-permute-done.3
  79.0 1.6 pad_maximum_fusion.1
  80.7 0.0 copy-start.3
  80.7 2.5 fusion.26
  83.1 1.6 multiply_reduce_fusion
  84.8 0.7 add.287
  85.5 0.0 all-reduce.4.cloned.1.call-update
  85.5 254.8 %all-reduce.4.cloned.1.call-done = f32[8,64,128]{2,1,0:T(8,128)} async-done(((f32[8,64,128]{2,1,0:T(8,128)}), f32[8,64,128]{2,1,0:T(8,128)}) %all-reduce.4.cloned.1.call-update) | async-done | bytes 262160 | tf_op jit(solution)/shard_map/psum | solution.py:107
  340.3 1.7 copy.30
  (31 shorter events, 0.3 us)
Async XLA Ops:
  7.2 8.3 %copy-start.7 = (f32[2,2,256]{2,1,0:T(2,128)S(1)}, f32[2,2,256]{2,1,0:T(2,128)}, u32[]{:S(2)}) copy-start(f32[2,2,256]{2,1,0:T(2,128)} %param.19) | copy-start | bytes 12292
  7.2 8.3 %copy-start.6 = (s32[2,256]{1,0:T(2,128)S(1)}, s32[2,256]{1,0:T(2,128)}, u32[]{:S(2)}) copy-start(s32[2,256]{1,0:T(2,128)} %param.25) | copy-start | bytes 6148
  7.2 8.3 %copy-start.8 = (f32[2,2]{1,0:T(2,128)S(1)}, f32[2,2]{1,0:T(2,128)}, u32[]{:S(2)}) copy-start(f32[2,2]{1,0:T(2,128)} %param.18) | copy-start | bytes 52
  7.2 8.3 %copy-start.9 = (s32[2]{0:T(128)S(1)}, s32[2]{0:T(128)}, u32[]{:S(2)}) copy-start(s32[2]{0:T(128)} %param.20) | copy-start | bytes 28
  7.2 8.3 %copy-start.11 = (s32[2]{0:T(128)S(1)}, s32[2]{0:T(128)}, u32[]{:S(2)}) copy-start(s32[2]{0:T(128)} %param.21) | copy-start | bytes 28
  7.2 8.3 %copy-start.10 = (s32[2]{0:T(128)S(1)}, s32[2]{0:T(128)}, u32[]{:S(2)}) copy-start(s32[2]{0:T(128)} %param.22) | copy-start | bytes 28
  7.2 333.1 %all-reduce.4.cloned.1.call-start = ((), (), s32[]{:S(2)}) async-start(), calls=%async_computation | async-start | bytes 524288 | tf_op jit(solution)/shard_map/psum | solution.py:107
  9.5 33.0 %collective-permute-start = (f32[2,2,4,64,128]{4,3,2,1,0:T(8,128)}, f32[2,2,4,64,128]{4,3,2,1,0:T(8,128)S(1)}, u32[]{:S(2)}, u32[]{:S(2)}) collective-permute-start(f32[2,2,4,64,128]{4,3,2,1,0:T(8,128)} %get-tuple-element.20), channel_id=1, source_target_pairs={{16,0},{32,16},{48,32},{64,48},{80,64},{96,80},{112,96},{128,112},... | collective-permute-start | bytes 1572872 | tf_op jit(solution)/shard_map/ppermute | solution.py:18
  10.8 31.7 %collective-permute-start.1 = (f32[2,2,4,64,128]{4,3,2,1,0:T(8,128)}, f32[2,2,4,64,128]{4,3,2,1,0:T(8,128)S(1)}, u32[]{:S(2)}, u32[]{:S(2)}) collective-permute-start(f32[2,2,4,64,128]{4,3,2,1,0:T(8,128)} %get-tuple-element.21), channel_id=1, source_target_pairs={{0,16},{16,32},{32,48},{48,64},{64,80},{80,96},{96,112},{112,128},... | collective-permute-start | bytes 1572872 | tf_op jit(solution)/shard_map/ppermute | solution.py:15
  16.9 24.9 %copy-start.12 = (s32[2]{0:T(128)S(1)}, s32[2]{0:T(128)}, u32[]{:S(2)}) copy-start(s32[2]{0:T(128)} %param.24) | copy-start | bytes 28
  16.9 25.0 %copy-start = (f32[2,8,64,128]{3,2,1,0:T(8,128)S(1)}, f32[2,8,64,128]{3,2,1,0:T(8,128)}, u32[]{:S(2)}) copy-start(f32[2,8,64,128]{3,2,1,0:T(8,128)} %param.14) | copy-start | bytes 1572868
  16.9 25.0 %copy-start.1 = (f32[2,8,64,128]{3,2,1,0:T(8,128)S(1)}, f32[2,8,64,128]{3,2,1,0:T(8,128)}, u32[]{:S(2)}) copy-start(f32[2,8,64,128]{3,2,1,0:T(8,128)} %param.16) | copy-start | bytes 1572868
  41.7 0.7 copy-start.13
  43.0 2.5 copy-start.2
  43.0 2.5 copy-start.4
  43.0 2.5 copy-start.5
  47.0 32.0 %collective-permute-start.2 = (f32[2,2,4,64,128]{4,3,2,1,0:T(8,128)}, f32[2,2,4,64,128]{4,3,2,1,0:T(8,128)}, u32[]{:S(2)}, u32[]{:S(2)}) collective-permute-start(f32[2,2,4,64,128]{4,3,2,1,0:T(8,128)} %get-tuple-element.16), channel_id=1, source_target_pairs={{16,0},{32,16},{48,32},{64,48},{80,64},{96,80},{112,96},{128,112},... | collective-permute-start | bytes 1572872 | tf_op jit(solution)/shard_map/ppermute | solution.py:18
  48.3 30.7 %collective-permute-start.3 = (f32[2,2,4,64,128]{4,3,2,1,0:T(8,128)}, f32[2,2,4,64,128]{4,3,2,1,0:T(8,128)}, u32[]{:S(2)}, u32[]{:S(2)}) collective-permute-start(f32[2,2,4,64,128]{4,3,2,1,0:T(8,128)} %get-tuple-element.17), channel_id=1, source_target_pairs={{0,16},{16,32},{32,48},{48,64},{64,80},{80,96},{96,112},{112,128},... | collective-permute-start | bytes 1572872 | tf_op jit(solution)/shard_map/ppermute | solution.py:15
  80.7 2.5 copy-start.3
Sparse Core Ops, SparseCore 0:
  85.6 254.6 all-reduce.3
where the time goes:
time: 349 us
  waiting for transfers between devices  255 us (73%)
  other arithmetic  64.6 us (19%)
  between operations  14.5 us (4%)
  starting transfers between devices  12 us (3%)
    psum x1, waiting for transfers between devices, per_device(): image = lax.psum(local_sum, 'shots')  255 us
    scatter-add x4, other arithmetic, inject(): jnp.zeros((count, length * plane), jnp.float32).at[rows, flat].add(amounts)  50.8 us
    ppermute x2, starting transfers between devices, extended(): lax.ppermute(lax.slice_in_dim(block, block.shape[dim] - width, None, axis...  9.39 us
  transfers between devices with their start and end apart: 5, of which 1 were waited for; matrix products, arithmetic and copies ran while one was open for 15% of the time, Pallas kernels for 0%

commit v1 on v0

--- a/solution.py
+++ b/solution.py
@@ -104,7 +104,7 @@
     local_sum = terms[0]
     for extra in terms[1:]:
         local_sum = local_sum + extra
-    image = lax.psum(local_sum, "shots")
+    image = jnp.sum(lax.all_gather(local_sum, "shots"), axis=0)
     return (src_last, rcv_last, image)
 
 

time: 349 us -> 261 us (0.75)
  waiting for transfers between devices: 255 us -> 164 us
    psum x1 -> x0, waiting for transfers between devices: 255 us -> none  [per_device(): image = lax.psum(local_sum, 'shots')]
    all_gather x0 -> x1, waiting for transfers between devices: none -> 164 us  [per_device(): image = jnp.sum(lax.all_gather(local_sum, 'shots'), axis=0)]
  transfers between devices with their start and end apart: 5 -> 5, of which waited for: 1 -> 1; matrix products, arithmetic and copies ran while one was open for 15% -> 20% of each run, Pallas kernels for 0% -> 0%
where the time goes in v1:
time: 261 us; the launch traced here: 260 us
  waiting for transfers between devices  164 us (63%)
  other arithmetic  67.7 us (26%)
  between operations  14.5 us (6%)
  starting transfers between devices  12 us (5%)
    all_gather x1, waiting for transfers between devices, per_device(): image = jnp.sum(lax.all_gather(local_sum, 'shots'), axis=0)  164 us
    scatter-add x4, other arithmetic, inject(): jnp.zeros((count, length * plane), jnp.float32).at[rows, flat].add(amounts)  50.8 us
    ppermute x2, starting transfers between devices, extended(): lax.ppermute(lax.slice_in_dim(block, block.shape[dim] - width, None, axis...  9.39 us
  transfers between devices with their start and end apart: 5, of which 1 were waited for; matrix products, arithmetic and copies ran while one was open for 20% of the time, Pallas kernels for 0%

profile of v1, /device:TPU:1, one launch (start us, length us, event | category | flops | bytes accessed | tf_op | source)
XLA Modules:
  0.0 259.6 jit_solution(3497826345116781391)
XLA Ops:
  7.2 0.0 copy-start.7
  7.2 0.0 copy-start.6
  7.2 0.0 copy-start.8
  7.2 0.0 all-gather.3.cloned.1.call-start
  7.3 2.3 fusion.58
  9.5 1.3 collective-permute-start
  10.8 4.6 %collective-permute-start.1 = (f32[2,2,4,64,128]{4,3,2,1,0:T(8,128)}, f32[2,2,4,64,128]{4,3,2,1,0:T(8,128)S(1)}, u32[]{:S(2)}, u32[]{:S(2)}) collective-permute-start(f32[2,2,4,64,128]{4,3,2,1,0:T(8,128)} %get-tuple-element.21), channel_id=1, source_target_pairs={{0,16},{16,32},{32,48},{48,64},{64,80},{80,96},{96,112},{112,128},... | collective-permute-start | bytes 1572872 | tf_op jit(solution)/shard_map/ppermute | solution.py:15
  15.6 0.1 copy.18
  15.7 0.2 fusion.83
  15.9 0.1 broadcast.180.clone.1
  16.1 0.6 scatter_fusion
  16.8 0.1 broadcast.180.clone
  16.9 0.0 copy-start.12
  16.9 0.0 copy-start
  16.9 0.0 copy-start.1
  16.9 24.8 %scatter_fusion.1 = f32[2,65536]{1,0:T(2,128)S(1)} fusion(f32[2,65536]{1,0:T(2,128)S(1)} %broadcast.180.clone, s32[512]{0:T(512)S(1)} %bitcast.88, f32[512]{0:T(512)S(1)} %bitcast.113), kind=kCustom, calls=%fused_computation.1 | custom fusion | flops 512 | bytes 10240 | tf_op jit(solution)/shard_map/scatter-add | solution.py:67
  41.7 0.0 copy-start.13
  41.8 0.1 abs_compare_fusion
  41.9 0.1 pad_maximum_fusion.2
  42.0 0.4 copy-done.13
  42.4 0.1 abs_compare_fusion.1
  42.5 0.1 and_convert_fusion
  42.6 0.0 collective-permute-done
  42.6 0.0 collective-permute-done.1
  42.6 0.4 pad_maximum_fusion
  43.0 0.0 copy-start.2
  43.0 0.0 copy-start.4
  43.0 0.0 copy-start.5
  43.0 2.5 fusion.6
  45.5 0.5 fusion.71
  46.0 1.0 fusion.56
  47.0 1.3 collective-permute-start.2
  48.3 4.8 %collective-permute-start.3 = (f32[2,2,4,64,128]{4,3,2,1,0:T(8,128)}, f32[2,2,4,64,128]{4,3,2,1,0:T(8,128)}, u32[]{:S(2)}, u32[]{:S(2)}) collective-permute-start(f32[2,2,4,64,128]{4,3,2,1,0:T(8,128)} %get-tuple-element.17), channel_id=1, source_target_pairs={{0,16},{16,32},{32,48},{48,64},{64,80},{80,96},{96,112},{112,128},... | collective-permute-start | bytes 1572872 | tf_op jit(solution)/shard_map/ppermute | solution.py:15
  53.1 0.1 broadcast.180.clone.3
  53.3 0.6 scatter_fusion.2
  54.0 0.1 broadcast.180.clone.2
  54.1 24.8 %scatter_fusion.3 = f32[2,65536]{1,0:T(2,128)S(1)} fusion(f32[2,65536]{1,0:T(2,128)S(1)} %broadcast.180.clone.2, s32[512]{0:T(512)S(1)} %bitcast.89, f32[512]{0:T(512)S(1)} %bitcast.112), kind=kCustom, calls=%fused_computation.3 | custom fusion | flops 512 | bytes 10240 | tf_op jit(solution)/shard_map/scatter-add | solution.py:67
  78.9 0.1 pad_maximum_fusion.3
  79.0 0.0 collective-permute-done.2
  79.0 0.0 collective-permute-done.3
  79.0 1.6 pad_maximum_fusion.1
  80.7 0.0 copy-start.3
  80.7 2.5 fusion.26
  83.1 1.6 multiply_reduce_fusion
  84.8 0.7 add.295
  85.5 0.0 all-gather.3.cloned.1.call-update
  85.5 164.1 %all-gather.3.cloned.1.call-done = f32[128,64,128]{2,1,0:T(8,128)} async-done(((f32[8,64,128]{2,1,0:T(8,128)}), f32[128,64,128]{2,1,0:T(8,128)}) %all-gather.3.cloned.1.call-update) | async-done | bytes 4194320 | tf_op jit(solution)/shard_map/all_gather | solution.py:107
  249.6 3.2 %reduce_sum.29 = f32[8,64,128]{2,1,0:T(8,128)} reduce(f32[16,8,64,128]{3,2,1,0:T(8,128)} %bitcast.106, f32[]{:T(128)} %constant.62.clone.1), dimensions={0}, to_apply=%region_6.7 | reduce | flops 983040 | bytes 4456452 | tf_op jit(solution)/shard_map/reduce_sum | solution.py:107
  (31 shorter events, 0.3 us)
Async XLA Ops:
  7.2 8.3 %copy-start.7 = (f32[2,2,256]{2,1,0:T(2,128)S(1)}, f32[2,2,256]{2,1,0:T(2,128)}, u32[]{:S(2)}) copy-start(f32[2,2,256]{2,1,0:T(2,128)} %param.19) | copy-start | bytes 12292
  7.2 8.3 %copy-start.6 = (s32[2,256]{1,0:T(2,128)S(1)}, s32[2,256]{1,0:T(2,128)}, u32[]{:S(2)}) copy-start(s32[2,256]{1,0:T(2,128)} %param.25) | copy-start | bytes 6148
  7.2 8.3 %copy-start.8 = (f32[2,2]{1,0:T(2,128)S(1)}, f32[2,2]{1,0:T(2,128)}, u32[]{:S(2)}) copy-start(f32[2,2]{1,0:T(2,128)} %param.18) | copy-start | bytes 52
  7.2 8.3 %copy-start.9 = (s32[2]{0:T(128)S(1)}, s32[2]{0:T(128)}, u32[]{:S(2)}) copy-start(s32[2]{0:T(128)} %param.20) | copy-start | bytes 28
  7.2 8.3 %copy-start.11 = (s32[2]{0:T(128)S(1)}, s32[2]{0:T(128)}, u32[]{:S(2)}) copy-start(s32[2]{0:T(128)} %param.21) | copy-start | bytes 28
  7.2 8.3 %copy-start.10 = (s32[2]{0:T(128)S(1)}, s32[2]{0:T(128)}, u32[]{:S(2)}) copy-start(s32[2]{0:T(128)} %param.22) | copy-start | bytes 28
  7.2 242.4 %all-gather.3.cloned.1.call-start = ((), (), s32[]{:S(2)}) async-start(), calls=%async_computation | async-start | bytes 4456448 | tf_op jit(solution)/shard_map/all_gather | solution.py:107
  9.5 33.0 %collective-permute-start = (f32[2,2,4,64,128]{4,3,2,1,0:T(8,128)}, f32[2,2,4,64,128]{4,3,2,1,0:T(8,128)S(1)}, u32[]{:S(2)}, u32[]{:S(2)}) collective-permute-start(f32[2,2,4,64,128]{4,3,2,1,0:T(8,128)} %get-tuple-element.20), channel_id=1, source_target_pairs={{16,0},{32,16},{48,32},{64,48},{80,64},{96,80},{112,96},{128,112},... | collective-permute-start | bytes 1572872 | tf_op jit(solution)/shard_map/ppermute | solution.py:18
  10.8 31.7 %collective-permute-start.1 = (f32[2,2,4,64,128]{4,3,2,1,0:T(8,128)}, f32[2,2,4,64,128]{4,3,2,1,0:T(8,128)S(1)}, u32[]{:S(2)}, u32[]{:S(2)}) collective-permute-start(f32[2,2,4,64,128]{4,3,2,1,0:T(8,128)} %get-tuple-element.21), channel_id=1, source_target_pairs={{0,16},{16,32},{32,48},{48,64},{64,80},{80,96},{96,112},{112,128},... | collective-permute-start | bytes 1572872 | tf_op jit(solution)/shard_map/ppermute | solution.py:15
  16.9 24.9 %copy-start.12 = (s32[2]{0:T(128)S(1)}, s32[2]{0:T(128)}, u32[]{:S(2)}) copy-start(s32[2]{0:T(128)} %param.24) | copy-start | bytes 28
  16.9 25.0 %copy-start = (f32[2,8,64,128]{3,2,1,0:T(8,128)S(1)}, f32[2,8,64,128]{3,2,1,0:T(8,128)}, u32[]{:S(2)}) copy-start(f32[2,8,64,128]{3,2,1,0:T(8,128)} %param.14) | copy-start | bytes 1572868
  16.9 25.0 %copy-start.1 = (f32[2,8,64,128]{3,2,1,0:T(8,128)S(1)}, f32[2,8,64,128]{3,2,1,0:T(8,128)}, u32[]{:S(2)}) copy-start(f32[2,8,64,128]{3,2,1,0:T(8,128)} %param.16) | copy-start | bytes 1572868
  41.7 0.7 copy-start.13
  43.0 2.5 copy-start.2
  43.0 2.5 copy-start.4
  43.0 2.5 copy-start.5
  47.0 32.0 %collective-permute-start.2 = (f32[2,2,4,64,128]{4,3,2,1,0:T(8,128)}, f32[2,2,4,64,128]{4,3,2,1,0:T(8,128)}, u32[]{:S(2)}, u32[]{:S(2)}) collective-permute-start(f32[2,2,4,64,128]{4,3,2,1,0:T(8,128)} %get-tuple-element.16), channel_id=1, source_target_pairs={{16,0},{32,16},{48,32},{64,48},{80,64},{96,80},{112,96},{128,112},... | collective-permute-start | bytes 1572872 | tf_op jit(solution)/shard_map/ppermute | solution.py:18
  48.3 30.7 %collective-permute-start.3 = (f32[2,2,4,64,128]{4,3,2,1,0:T(8,128)}, f32[2,2,4,64,128]{4,3,2,1,0:T(8,128)}, u32[]{:S(2)}, u32[]{:S(2)}) collective-permute-start(f32[2,2,4,64,128]{4,3,2,1,0:T(8,128)} %get-tuple-element.17), channel_id=1, source_target_pairs={{0,16},{16,32},{32,48},{48,64},{64,80},{80,96},{96,112},{112,128},... | collective-permute-start | bytes 1572872 | tf_op jit(solution)/shard_map/ppermute | solution.py:15
  80.7 2.5 copy-start.3
Sparse Core Ops, SparseCore 0:
  85.6 163.9 all-gather.2
